TPU v7x, 256 devices: a whole 4x4x8 slice. The times are simulated.
256 devices in a mesh: slab: 32 (over y, z), mode: 8 (over x, core).
Axes of the slice: x: 4, y: 4, z: 8, core: 2. Of those that a mesh axis runs over, the one named last changes fastest.
Arguments:
- positions: float32 [3, 524288], P(None, ('slab', 'mode')), may hold values from 0 to 1, as said below
- charges: float32 [524288], P(('slab', 'mode')), may hold values from -0.03125 to 0.03125
- counts: int32 [32], replicated, may hold values from 3840 to 16384, as said below
- box: float32 [2], replicated, may hold values from 0.8 to 1.25
Outputs:
- forces: float32 [3, 524288], P(None, ('slab', 'mode'))
Inputs may be any that keep to these rules, and one draw needn't show every extreme that they name: positions[0] and positions[1] are fractional coordinates; positions[2, i] lies strictly between s 0.08 / 32 and (s + 1) 0.08 / 32 for s = i // 16384, and never falls with i within a slab. The live ions of a slab are its first counts[s] slots; some slab is full.
All inputs are finite; a program needn't handle non-finite values.
Results may differ from a plain program's by a relative error of at most 0.0003.
Values sent between devices are 32-bit elements; how exact they have to be, the bound alone decides.
A program may use at most 64 MiB of HBM per device.

v0:
```python
import math
import jax
import jax.numpy as jnp
from jax import lax
from jax.sharding import PartitionSpec as P

QDIM = 64
BLOCK = 512
MODES = 4096
two_pi = 2.0 * math.pi
slab_span = 0.08


def carried_in(value, axis, combine, identity, reverse):
    size, mine = (lax.axis_size(axis), lax.axis_index(axis))
    everything = jax.tree.map(lambda part: lax.all_gather(part, axis), value)
    start = jax.tree.map(
        lambda part, zero: jnp.broadcast_to(jnp.asarray(zero, part.dtype), part.shape),
        value,
        identity,
    )

    def lap(k, before):
        at = size - 1 - k if reverse else k
        reached = at > mine if reverse else at < mine
        new = combine(before, jax.tree.map(lambda part: part[at], everything))
        return jax.tree.map(lambda a, b: jnp.where(reached, a, b), new, before)

    return lax.fori_loop(0, size, lap, start)


def wave_table(first_mode, mode_count, box):
    mode_index = first_mode + jnp.arange(mode_count, dtype=jnp.int32)
    order_p = (mode_index // QDIM + 1).astype(jnp.float32)
    order_q = (mode_index % QDIM - QDIM // 2).astype(jnp.float32)
    wave_x = two_pi * order_p / box[0]
    wave_y = two_pi * order_q / box[1]
    wave_norm = jnp.sqrt(wave_x * wave_x + wave_y * wave_y)
    return (order_p, order_q, wave_x / wave_norm, wave_y / wave_norm, wave_norm)


def phase_terms(mode_info, coords, lower_edge, height):
    order_p, order_q, unit_x, unit_y, wave_norm = mode_info
    phase_angle = two_pi * (
        order_p[:, None] * coords[0][None, :] + order_q[:, None] * coords[1][None, :]
    )
    ion_depth = coords[2][None, :] - lower_edge
    e_low = jnp.exp(-wave_norm[:, None] * ion_depth)
    e_high = jnp.exp(-wave_norm[:, None] * (height - ion_depth))
    return (jnp.cos(phase_angle), jnp.sin(phase_angle), e_low, e_high)


def block_moments(mode_info, coords, weight, lower_edge, height):
    cosine, sine_part, e_low, e_high = phase_terms(mode_info, coords, lower_edge, height)
    upward = weight[None, :] * e_high
    downward = weight[None, :] * e_low
    row_stack = jnp.stack(
        [upward * cosine, upward * sine_part, downward * cosine, downward * sine_part]
    )
    mode_count = cosine.shape[0]
    return jnp.sum(row_stack.reshape(4, mode_count, cosine.shape[1] // BLOCK, BLOCK), axis=3)


def force_terms(mode_info, coords, weight, coefficients, lower_edge, height, box):
    order_p, order_q, unit_x, unit_y, wave_norm = mode_info
    cosine, sine_part, e_low, e_high = phase_terms(mode_info, coords, lower_edge, height)
    mode_count, ion_count = cosine.shape
    block_count = coefficients.shape[2]

    def spread(row_values):
        return jnp.broadcast_to(row_values[:, :, None], (mode_count, block_count, BLOCK)).reshape(
            mode_count, ion_count
        )

    below_c = e_low * spread(coefficients[0])
    below_s = e_low * spread(coefficients[1])
    above_c = e_high * spread(coefficients[2])
    above_s = e_high * spread(coefficients[3])
    in_plane = sine_part * (below_c + above_c) - cosine * (below_s + above_s)
    normal = cosine * (below_c - above_c) + sine_part * (below_s - above_s)
    scale = 2.0 * two_pi / (box[0] * box[1]) * weight
    return (
        jnp.stack(
            [
                jnp.sum(unit_x[:, None] * in_plane, axis=0),
                jnp.sum(unit_y[:, None] * in_plane, axis=0),
                jnp.sum(normal, axis=0),
            ]
        )
        * scale[None, :]
    )


def group_blocks(ion_total):
    block_count = ion_total // BLOCK
    chosen = 1
    for factor in range(1, 5):
        if block_count % factor == 0:
            chosen = factor
    return chosen


def sweep_moments(mode_info, coords, weight, lower_edge, height):
    ion_total = coords.shape[1]
    per_group = group_blocks(ion_total)
    group_width = per_group * BLOCK
    group_count = ion_total // group_width
    coord_groups = coords.reshape(3, group_count, group_width).transpose(1, 0, 2)
    weight_groups = weight.reshape(group_count, group_width)

    def advance(carried, group_item):
        return (carried, block_moments(mode_info, group_item[0], group_item[1], lower_edge, height))

    _, pieces = lax.scan(advance, jnp.int32(0), (coord_groups, weight_groups))
    mode_count = pieces.shape[2]
    return pieces.transpose(1, 2, 0, 3).reshape(4, mode_count, group_count * per_group)


def sweep_forces(mode_info, coords, weight, coefficients, lower_edge, height, box):
    ion_total = coords.shape[1]
    per_group = group_blocks(ion_total)
    group_width = per_group * BLOCK
    group_count = ion_total // group_width
    mode_count = coefficients.shape[1]
    coord_groups = coords.reshape(3, group_count, group_width).transpose(1, 0, 2)
    weight_groups = weight.reshape(group_count, group_width)
    coeff_groups = coefficients.reshape(4, mode_count, group_count, per_group).transpose(2, 0, 1, 3)

    def advance(carried, group_item):
        return (
            carried,
            force_terms(
                mode_info, group_item[0], group_item[1], group_item[2], lower_edge, height, box
            ),
        )

    _, pieces = lax.scan(advance, jnp.int32(0), (coord_groups, weight_groups, coeff_groups))
    return pieces.transpose(1, 0, 2).reshape(3, ion_total)


def carry_coefficients(moments, wave_norm, height):
    mode_count = moments.shape[1]
    block_count = moments.shape[2]
    block_ids = jnp.arange(block_count, dtype=jnp.int32)
    lower_tri = (block_ids[:, None] < block_ids[None, :]).astype(jnp.float32)
    upper_tri = (block_ids[:, None] > block_ids[None, :]).astype(jnp.float32)
    prefix_up = jnp.dot(
        moments[0:2].reshape(2 * mode_count, block_count),
        lower_tri,
        precision=lax.Precision.HIGHEST,
    ).reshape(2, mode_count, block_count)
    suffix_down = jnp.dot(
        moments[2:4].reshape(2 * mode_count, block_count),
        upper_tri,
        precision=lax.Precision.HIGHEST,
    ).reshape(2, mode_count, block_count)
    totals = jnp.sum(moments, axis=2)
    decay_step = jnp.exp(-wave_norm * height)

    def compose(earlier, later):
        return (earlier[0] * later[0], earlier[1] * later[0][None, :] + later[1])

    identity = (jnp.ones_like(decay_step), jnp.zeros((2, mode_count), jnp.float32))
    _, carry_up = carried_in((decay_step, totals[0:2]), "slab", compose, identity, False)
    _, carry_down = carried_in((decay_step, totals[2:4]), "slab", compose, identity, True)
    boost_step = jnp.exp(wave_norm * height)[None, :, None]
    return jnp.concatenate(
        [
            carry_up[:, :, None] + boost_step * prefix_up,
            carry_down[:, :, None] + boost_step * suffix_down,
        ],
        axis=0,
    )


def shards(positions, charges, counts, box):
    slab_count = lax.axis_size("slab")
    mode_parts = lax.axis_size("mode")
    slab_rank = lax.axis_index("slab")
    mode_rank = lax.axis_index("mode")
    modes_dev = MODES // mode_parts
    height = slab_span / slab_count
    lower_edge = slab_rank.astype(jnp.float32) * height
    live_count = jnp.sum(jnp.where(jnp.arange(slab_count, dtype=jnp.int32) == slab_rank, counts, 0))
    coords, charge = (
        lax.all_gather(positions, "mode", axis=1, tiled=True),
        lax.all_gather(charges, "mode", axis=0, tiled=True),
    )
    live_mask = jnp.arange(coords.shape[1], dtype=jnp.int32) < live_count
    weight = jnp.where(live_mask, charge, jnp.float32(0.0))
    mode_info = wave_table(mode_rank * modes_dev, modes_dev, box)
    moments = sweep_moments(mode_info, coords, weight, lower_edge, height)
    coefficients = carry_coefficients(moments, mode_info[4], height)
    partial_force = sweep_forces(mode_info, coords, weight, coefficients, lower_edge, height, box)
    return lax.psum_scatter(partial_force, "mode", scatter_dimension=1, tiled=True)


def solution(mesh):
    return jax.shard_map(
        shards,
        mesh=mesh,
        in_specs=(P(None, ("slab", "mode")), P(("slab", "mode")), P(), P()),
        out_specs=P(None, ("slab", "mode")),
        check_vma=False,
    )
```

profile of v0, /device:TPU:1, one launch (start us, length us, event | category | flops | bytes accessed | tf_op | source)
XLA Modules:
  0.0 587.2 jit_solution(16965568512662683384)
XLA Ops:
  6.5 1.4 fusion.79
  7.9 1.3 exponential_bitcast_fusion
  9.2 1.3 multiply_exponential_fusion.2
  11.8 1.4 fusion.77
  13.1 16.0 %all_gather.26 = f32[16384]{0:T(1024)S(1)} all-gather(f32[2048]{0:T(1024)} %param.13), channel_id=1, replica_groups=mesh['slab'=32,'mode'=8] {'mode'}, dimensions={0}, use_global_device_ids=true | all-gather | bytes 73728 | tf_op jit(solution)/shard_map/all_gather | solution.py:187
  29.8 13.1 %all_gather.24 = f32[3,16384]{1,0:T(4,128)S(1)} all-gather(f32[3,2048]{1,0:T(4,128)} %param.12), channel_id=1, replica_groups=mesh['slab'=32,'mode'=8] {'mode'}, dimensions={1}, use_global_device_ids=true | all-gather | bytes 221184 | tf_op jit(solution)/shard_map/all_gather | solution.py:186
  42.9 161.3 %while.60 = (s32[]{:T(128)}, f32[8,4,512,4]{2,3,1,0:T(4,128)S(1)}, f32[8,2048]{1,0:T(8,128)S(1)}, f32[8,3,2048]{2,1,0:T(4,128)S(1)}, f32[]{:T(128)}, /*index=5*/...) while((s32[]{:T(128)}, f32[8,4,512,4]{2,3,1,0:T(4,128)S(1)}, ...), condition=%wide.region_3.4_spmd.clone.clone, body=%wide.region_1.3_spmd.clone.clone.sunk | while | flops 29384708 | bytes 33853620 | solution.py:114
  43.0 1.3 sqrt_negate_fusion.4
  44.3 17.2 %fusion.91 = (f32[1,512,4,512]{3,1,2,0:T(8,128)S(1)}, f32[1,512,4,512]{3,1,2,0:T(8,128)S(1)}, f32[1,512,4,512]{3,1,2,0:T(8,128)S(1)}, f32[1,512,4,512]{3,1,2,0:T(8,128)S(1)}) fusion(f32[4,512]{1,0:T(4,128)S(1)} %mul.1380, f32[512]{0:T(512)S(1)} %get-tuple-element.909, f32[4,512]{1,0:T(4,128)S(1)} %mul.1381, f32[512]{0:T(512)S(1)} %get-tuple-element.911, ...), kind=kLoop, calls=%fused_computation.21.clone.1 | loop fusion | flops 12582912 | bytes 16824320 | tf_op jit(solution)/shard_map/while/body/eval_jaxpr/mul | solution.py:58
  61.5 1.4 maximum_reduce_fusion.2
  63.2 1.3 sqrt_negate_fusion.4
  64.5 17.2 %fusion.91 = (f32[1,512,4,512]{3,1,2,0:T(8,128)S(1)}, f32[1,512,4,512]{3,1,2,0:T(8,128)S(1)}, f32[1,512,4,512]{3,1,2,0:T(8,128)S(1)}, f32[1,512,4,512]{3,1,2,0:T(8,128)S(1)}) fusion(f32[4,512]{1,0:T(4,128)S(1)} %mul.1380, f32[512]{0:T(512)S(1)} %get-tuple-element.909, f32[4,512]{1,0:T(4,128)S(1)} %mul.1381, f32[512]{0:T(512)S(1)} %get-tuple-element.911, ...), kind=kLoop, calls=%fused_computation.21.clone.1 | loop fusion | flops 12582912 | bytes 16824320 | tf_op jit(solution)/shard_map/while/body/eval_jaxpr/mul | solution.py:58
  81.7 1.4 maximum_reduce_fusion.2
  83.4 1.3 sqrt_negate_fusion.4
  84.7 17.2 %fusion.91 = (f32[1,512,4,512]{3,1,2,0:T(8,128)S(1)}, f32[1,512,4,512]{3,1,2,0:T(8,128)S(1)}, f32[1,512,4,512]{3,1,2,0:T(8,128)S(1)}, f32[1,512,4,512]{3,1,2,0:T(8,128)S(1)}) fusion(f32[4,512]{1,0:T(4,128)S(1)} %mul.1380, f32[512]{0:T(512)S(1)} %get-tuple-element.909, f32[4,512]{1,0:T(4,128)S(1)} %mul.1381, f32[512]{0:T(512)S(1)} %get-tuple-element.911, ...), kind=kLoop, calls=%fused_computation.21.clone.1 | loop fusion | flops 12582912 | bytes 16824320 | tf_op jit(solution)/shard_map/while/body/eval_jaxpr/mul | solution.py:58
  101.9 1.4 maximum_reduce_fusion.2
  103.5 1.3 sqrt_negate_fusion.4
  104.8 17.2 %fusion.91 = (f32[1,512,4,512]{3,1,2,0:T(8,128)S(1)}, f32[1,512,4,512]{3,1,2,0:T(8,128)S(1)}, f32[1,512,4,512]{3,1,2,0:T(8,128)S(1)}, f32[1,512,4,512]{3,1,2,0:T(8,128)S(1)}) fusion(f32[4,512]{1,0:T(4,128)S(1)} %mul.1380, f32[512]{0:T(512)S(1)} %get-tuple-element.909, f32[4,512]{1,0:T(4,128)S(1)} %mul.1381, f32[512]{0:T(512)S(1)} %get-tuple-element.911, ...), kind=kLoop, calls=%fused_computation.21.clone.1 | loop fusion | flops 12582912 | bytes 16824320 | tf_op jit(solution)/shard_map/while/body/eval_jaxpr/mul | solution.py:58
  122.0 1.4 maximum_reduce_fusion.2
  123.7 1.3 sqrt_negate_fusion.4
  125.0 17.2 %fusion.91 = (f32[1,512,4,512]{3,1,2,0:T(8,128)S(1)}, f32[1,512,4,512]{3,1,2,0:T(8,128)S(1)}, f32[1,512,4,512]{3,1,2,0:T(8,128)S(1)}, f32[1,512,4,512]{3,1,2,0:T(8,128)S(1)}) fusion(f32[4,512]{1,0:T(4,128)S(1)} %mul.1380, f32[512]{0:T(512)S(1)} %get-tuple-element.909, f32[4,512]{1,0:T(4,128)S(1)} %mul.1381, f32[512]{0:T(512)S(1)} %get-tuple-element.911, ...), kind=kLoop, calls=%fused_computation.21.clone.1 | loop fusion | flops 12582912 | bytes 16824320 | tf_op jit(solution)/shard_map/while/body/eval_jaxpr/mul | solution.py:58
  142.2 1.4 maximum_reduce_fusion.2
  143.8 1.3 sqrt_negate_fusion.4
  145.2 17.2 %fusion.91 = (f32[1,512,4,512]{3,1,2,0:T(8,128)S(1)}, f32[1,512,4,512]{3,1,2,0:T(8,128)S(1)}, f32[1,512,4,512]{3,1,2,0:T(8,128)S(1)}, f32[1,512,4,512]{3,1,2,0:T(8,128)S(1)}) fusion(f32[4,512]{1,0:T(4,128)S(1)} %mul.1380, f32[512]{0:T(512)S(1)} %get-tuple-element.909, f32[4,512]{1,0:T(4,128)S(1)} %mul.1381, f32[512]{0:T(512)S(1)} %get-tuple-element.911, ...), kind=kLoop, calls=%fused_computation.21.clone.1 | loop fusion | flops 12582912 | bytes 16824320 | tf_op jit(solution)/shard_map/while/body/eval_jaxpr/mul | solution.py:58
  162.3 1.4 maximum_reduce_fusion.2
  164.0 1.3 sqrt_negate_fusion.4
  165.3 17.2 %fusion.91 = (f32[1,512,4,512]{3,1,2,0:T(8,128)S(1)}, f32[1,512,4,512]{3,1,2,0:T(8,128)S(1)}, f32[1,512,4,512]{3,1,2,0:T(8,128)S(1)}, f32[1,512,4,512]{3,1,2,0:T(8,128)S(1)}) fusion(f32[4,512]{1,0:T(4,128)S(1)} %mul.1380, f32[512]{0:T(512)S(1)} %get-tuple-element.909, f32[4,512]{1,0:T(4,128)S(1)} %mul.1381, f32[512]{0:T(512)S(1)} %get-tuple-element.911, ...), kind=kLoop, calls=%fused_computation.21.clone.1 | loop fusion | flops 12582912 | bytes 16824320 | tf_op jit(solution)/shard_map/while/body/eval_jaxpr/mul | solution.py:58
  182.5 1.4 maximum_reduce_fusion.2
  184.2 1.3 sqrt_negate_fusion.4
  185.5 17.2 %fusion.91 = (f32[1,512,4,512]{3,1,2,0:T(8,128)S(1)}, f32[1,512,4,512]{3,1,2,0:T(8,128)S(1)}, f32[1,512,4,512]{3,1,2,0:T(8,128)S(1)}, f32[1,512,4,512]{3,1,2,0:T(8,128)S(1)}) fusion(f32[4,512]{1,0:T(4,128)S(1)} %mul.1380, f32[512]{0:T(512)S(1)} %get-tuple-element.909, f32[4,512]{1,0:T(4,128)S(1)} %mul.1381, f32[512]{0:T(512)S(1)} %get-tuple-element.911, ...), kind=kLoop, calls=%fused_computation.21.clone.1 | loop fusion | flops 12582912 | bytes 16824320 | tf_op jit(solution)/shard_map/while/body/eval_jaxpr/mul | solution.py:58
  202.7 1.4 maximum_reduce_fusion.2
  204.2 35.3 %all-gather.3 = f32[32,2,512]{2,1,0:T(2,128)S(1)} all-gather(f32[1,2,512]{2,1,0:T(2,128)S(1)} %get-tuple-element.719), channel_id=2, replica_groups=mesh['slab'=32,'mode'=8] {'slab'}, dimensions={0}, use_global_device_ids=true | all-gather | bytes 135168 | tf_op jit(solution)/shard_map/all_gather | solution.py:16
  239.6 36.0 %all-gather.2 = f32[32,1,512]{2,1,0:T(1,128)S(1)} all-gather(f32[1,1,512]{2,1,0:T(1,128)S(1)} %exponential_bitcast_fusion), channel_id=1, replica_groups=mesh['slab'=32,'mode'=8] {'slab'}, dimensions={0}, use_global_device_ids=true | all-gather | bytes 67584 | tf_op jit(solution)/shard_map/all_gather | solution.py:16
  275.5 1.9 while.58
  277.5 31.4 %all-gather.4 = f32[32,2,512]{2,1,0:T(2,128)S(1)} all-gather(f32[1,2,512]{2,1,0:T(2,128)S(1)} %get-tuple-element.720), channel_id=3, replica_groups=mesh['slab'=32,'mode'=8] {'slab'}, dimensions={0}, use_global_device_ids=true | all-gather | bytes 135168 | tf_op jit(solution)/shard_map/all_gather | solution.py:16
  308.9 2.3 while.59
  311.8 178.5 %while.61 = (s32[]{:T(128)}, f32[8,3,2048]{2,1,0:T(4,128)S(1)}, f32[8,3,2048]{2,1,0:T(4,128)S(1)}, f32[]{:T(128)}, f32[8,4,512,4]{2,3,1,0:T(4,128)S(1)}, /*index...) while((s32[]{:T(128)}, f32[8,3,2048]{2,1,0:T(4,128)S(1)}, ...), condition=%wide.region_13.14_spmd.clone.clone, body=%wide.region_9.13_spmd.clone.clone.sunk | while | flops 26279428 | bytes 422137 | solution.py:137
  312.0 1.3 multiply_divide_fusion.3
  313.3 1.3 sqrt_negate_fusion.5
  314.6 19.4 %multiply_reduce_fusion.3 = (f32[4,512]{1,0:T(4,128)S(1)}, f32[4,512]{1,0:T(4,128)S(1)}, f32[4,512]{1,0:T(4,128)S(1)}) fusion(f32[512,4]{0,1:T(4,128)S(1)} %get-tuple-element.927, f32[512,4]{0,1:T(4,128)S(1)} %get-tuple-element.928, f32[512,4]{0,1:T(4,128)S(1)} %get-tuple-element.929, f32[4,512]{1,0:T(4,128)S(1)} %broadcast_subtract_fusion.5, ...), kind=kLoop, calls=%fused_computation.59.clone.1 | loop fusion | flops 26208256 | bytes 100352 | tf_op jit(solution)/shard_map/while/body/eval_jaxpr/reduce_sum | solution.py:85
  334.3 1.3 multiply_divide_fusion.3
  335.6 1.3 sqrt_negate_fusion.5
  336.9 19.4 %multiply_reduce_fusion.3 = (f32[4,512]{1,0:T(4,128)S(1)}, f32[4,512]{1,0:T(4,128)S(1)}, f32[4,512]{1,0:T(4,128)S(1)}) fusion(f32[512,4]{0,1:T(4,128)S(1)} %get-tuple-element.927, f32[512,4]{0,1:T(4,128)S(1)} %get-tuple-element.928, f32[512,4]{0,1:T(4,128)S(1)} %get-tuple-element.929, f32[4,512]{1,0:T(4,128)S(1)} %broadcast_subtract_fusion.5, ...), kind=kLoop, calls=%fused_computation.59.clone.1 | loop fusion | flops 26208256 | bytes 100352 | tf_op jit(solution)/shard_map/while/body/eval_jaxpr/reduce_sum | solution.py:85
  356.6 1.3 multiply_divide_fusion.3
  357.9 1.3 sqrt_negate_fusion.5
  359.2 19.4 %multiply_reduce_fusion.3 = (f32[4,512]{1,0:T(4,128)S(1)}, f32[4,512]{1,0:T(4,128)S(1)}, f32[4,512]{1,0:T(4,128)S(1)}) fusion(f32[512,4]{0,1:T(4,128)S(1)} %get-tuple-element.927, f32[512,4]{0,1:T(4,128)S(1)} %get-tuple-element.928, f32[512,4]{0,1:T(4,128)S(1)} %get-tuple-element.929, f32[4,512]{1,0:T(4,128)S(1)} %broadcast_subtract_fusion.5, ...), kind=kLoop, calls=%fused_computation.59.clone.1 | loop fusion | flops 26208256 | bytes 100352 | tf_op jit(solution)/shard_map/while/body/eval_jaxpr/reduce_sum | solution.py:85
  378.9 1.3 multiply_divide_fusion.3
  380.2 1.3 sqrt_negate_fusion.5
  381.5 19.4 %multiply_reduce_fusion.3 = (f32[4,512]{1,0:T(4,128)S(1)}, f32[4,512]{1,0:T(4,128)S(1)}, f32[4,512]{1,0:T(4,128)S(1)}) fusion(f32[512,4]{0,1:T(4,128)S(1)} %get-tuple-element.927, f32[512,4]{0,1:T(4,128)S(1)} %get-tuple-element.928, f32[512,4]{0,1:T(4,128)S(1)} %get-tuple-element.929, f32[4,512]{1,0:T(4,128)S(1)} %broadcast_subtract_fusion.5, ...), kind=kLoop, calls=%fused_computation.59.clone.1 | loop fusion | flops 26208256 | bytes 100352 | tf_op jit(solution)/shard_map/while/body/eval_jaxpr/reduce_sum | solution.py:85
  401.3 1.3 multiply_divide_fusion.3
  402.5 1.3 sqrt_negate_fusion.5
  403.8 19.4 %multiply_reduce_fusion.3 = (f32[4,512]{1,0:T(4,128)S(1)}, f32[4,512]{1,0:T(4,128)S(1)}, f32[4,512]{1,0:T(4,128)S(1)}) fusion(f32[512,4]{0,1:T(4,128)S(1)} %get-tuple-element.927, f32[512,4]{0,1:T(4,128)S(1)} %get-tuple-element.928, f32[512,4]{0,1:T(4,128)S(1)} %get-tuple-element.929, f32[4,512]{1,0:T(4,128)S(1)} %broadcast_subtract_fusion.5, ...), kind=kLoop, calls=%fused_computation.59.clone.1 | loop fusion | flops 26208256 | bytes 100352 | tf_op jit(solution)/shard_map/while/body/eval_jaxpr/reduce_sum | solution.py:85
  423.6 1.3 multiply_divide_fusion.3
  424.8 1.3 sqrt_negate_fusion.5
  426.2 19.4 %multiply_reduce_fusion.3 = (f32[4,512]{1,0:T(4,128)S(1)}, f32[4,512]{1,0:T(4,128)S(1)}, f32[4,512]{1,0:T(4,128)S(1)}) fusion(f32[512,4]{0,1:T(4,128)S(1)} %get-tuple-element.927, f32[512,4]{0,1:T(4,128)S(1)} %get-tuple-element.928, f32[512,4]{0,1:T(4,128)S(1)} %get-tuple-element.929, f32[4,512]{1,0:T(4,128)S(1)} %broadcast_subtract_fusion.5, ...), kind=kLoop, calls=%fused_computation.59.clone.1 | loop fusion | flops 26208256 | bytes 100352 | tf_op jit(solution)/shard_map/while/body/eval_jaxpr/reduce_sum | solution.py:85
  445.9 1.3 multiply_divide_fusion.3
  447.1 1.3 sqrt_negate_fusion.5
  448.5 19.4 %multiply_reduce_fusion.3 = (f32[4,512]{1,0:T(4,128)S(1)}, f32[4,512]{1,0:T(4,128)S(1)}, f32[4,512]{1,0:T(4,128)S(1)}) fusion(f32[512,4]{0,1:T(4,128)S(1)} %get-tuple-element.927, f32[512,4]{0,1:T(4,128)S(1)} %get-tuple-element.928, f32[512,4]{0,1:T(4,128)S(1)} %get-tuple-element.929, f32[4,512]{1,0:T(4,128)S(1)} %broadcast_subtract_fusion.5, ...), kind=kLoop, calls=%fused_computation.59.clone.1 | loop fusion | flops 26208256 | bytes 100352 | tf_op jit(solution)/shard_map/while/body/eval_jaxpr/reduce_sum | solution.py:85
  468.2 1.3 multiply_divide_fusion.3
  469.5 1.3 sqrt_negate_fusion.5
  470.8 19.4 %multiply_reduce_fusion.3 = (f32[4,512]{1,0:T(4,128)S(1)}, f32[4,512]{1,0:T(4,128)S(1)}, f32[4,512]{1,0:T(4,128)S(1)}) fusion(f32[512,4]{0,1:T(4,128)S(1)} %get-tuple-element.927, f32[512,4]{0,1:T(4,128)S(1)} %get-tuple-element.928, f32[512,4]{0,1:T(4,128)S(1)} %get-tuple-element.929, f32[4,512]{1,0:T(4,128)S(1)} %broadcast_subtract_fusion.5, ...), kind=kLoop, calls=%fused_computation.59.clone.1 | loop fusion | flops 26208256 | bytes 100352 | tf_op jit(solution)/shard_map/while/body/eval_jaxpr/reduce_sum | solution.py:85
  490.3 5.1 copy.33
  495.4 82.8 %reduce-scatter.4.cloned.1.call-done = f32[2048,3]{1,0:T(8,128)} async-done(((f32[16384,3]{1,0:T(8,128)}), f32[2048,3]{1,0:T(8,128)}) %reduce-scatter.4.cloned.1.call-update) | async-done | bytes 24592
  578.2 2.2 copy.34
  (317 shorter events, 6.7 us)
Async XLA Ops:
  6.5 571.7 %reduce-scatter.4.cloned.1.call-start = ((), (), s32[]{:S(2)}) async-start(), calls=%async_computation.1 | async-start | bytes 9437184
Sparse Core Ops, SparseCore 0:
  495.6 82.6 reduce-scatter.3
where the time goes:
time: 588 us; the launch traced here: 587 us
  other arithmetic  343 us (58%)
  blocking collectives  132 us (22%)
  waiting for transfers between devices  82.8 us (14%)
  between operations  14.9 us (3%)
  local copies, waits for them, and re-layouts  11.1 us (2%)
    reduce_sum x8, other arithmetic, force_terms(): jnp.sum(unit_x[:, None] * in_plane, axis=0)  155 us
    mul x8, other arithmetic, block_moments(): upward * cosine  137 us
    all_gather x3, blocking collectives, carried_in(): everything = jax.tree.map(lambda part: lax.all_gather(part, axis), value)  103 us
    unnamed x2, waiting for transfers between devices  82.8 us
    neg x16, other arithmetic, phase_terms(): e_high = jnp.exp(-wave_norm[:, None] * (height - ion_depth))  20.6 us
    all_gather x1, blocking collectives, shards(): lax.all_gather(charges, 'mode', axis=0, tiled=True)  16 us
    all_gather x1, blocking collectives, shards(): lax.all_gather(positions, 'mode', axis=1, tiled=True)  13.1 us
  transfers between devices with their start and end apart: 1, of which 1 were waited for; matrix products, arithmetic and copies ran while one was open for 0% of the time, Pallas kernels for 0%

commit v1 on v0

--- a/solution.py
+++ b/solution.py
@@ -184,7 +184,9 @@
     live_count = jnp.sum(jnp.where(jnp.arange(slab_count, dtype=jnp.int32) == slab_rank, counts, 0))
     coords, charge = (
         lax.all_gather(positions, "mode", axis=1, tiled=True),
-        lax.all_gather(charges, "mode", axis=0, tiled=True),
+        jnp.concatenate(
+            lax.all_to_all(jnp.stack([charges] * lax.axis_size("mode")), "mode", 0, 0), axis=0
+        ),
     )
     live_mask = jnp.arange(coords.shape[1], dtype=jnp.int32) < live_count
     weight = jnp.where(live_mask, charge, jnp.float32(0.0))

time: 588 us -> 580 us (0.986)
  waiting for transfers between devices: 82.8 us -> 71.1 us
  starting transfers between devices: 0.01 us -> 6.45 us
    all_gather x1 -> x0, blocking collectives: 16 us -> none  [shards(): lax.all_gather(charges, 'mode', axis=0, tiled=True)]
    all_gather x1, blocking collectives: 13.1 us -> 26.2 us  [shards(): lax.all_gather(positions, 'mode', axis=1, tiled=True)]
    unnamed x2, waiting for transfers between devices: 82.8 us -> 71.1 us
    all_to_all x0 -> x1, starting transfers between devices: none -> 6.45 us  [shards(): lax.all_to_all(jnp.stack([charges] * lax.axis_size('mode')), 'mode', 0, 0)]
  transfers between devices with their start and end apart: 1 -> 2, of which waited for: 1 -> 1; matrix products, arithmetic and copies ran while one was open for 0% -> 1% of each run, Pallas kernels for 0% -> 0%
where the time goes in v1:
time: 580 us
  other arithmetic  342 us (59%)
  blocking collectives  129 us (22%)
  waiting for transfers between devices  71.1 us (12%)
  between operations  14.8 us (3%)
  local copies, waits for them, and re-layouts  12.4 us (2%)
  starting transfers between devices  6.45 us (1%)
    reduce_sum x8, other arithmetic, force_terms(): jnp.sum(unit_x[:, None] * in_plane, axis=0)  155 us
    mul x8, other arithmetic, block_moments(): upward * cosine  137 us
    all_gather x3, blocking collectives, carried_in(): everything = jax.tree.map(lambda part: lax.all_gather(part, axis), value)  103 us
    unnamed x2, waiting for transfers between devices  71.1 us
    all_gather x1, blocking collectives, shards(): lax.all_gather(positions, 'mode', axis=1, tiled=True)  26.2 us
    neg x16, other arithmetic, phase_terms(): e_high = jnp.exp(-wave_norm[:, None] * (height - ion_depth))  20.2 us
  transfers between devices with their start and end apart: 2, of which 1 were waited for; matrix products, arithmetic and copies ran while one was open for 1% of the time, Pallas kernels for 0%

profile of v1, /device:TPU:1, one launch (start us, length us, event | category | flops | bytes accessed | tf_op | source)
XLA Modules:
  0.0 579.7 jit_solution(10222998891475443336)
XLA Ops:
  6.5 1.3 stack.12
  7.9 6.5 %all-to-all-start = ((f32[8,1,2048]{2,1,0:T(1,128)}), f32[8,1,2048]{2,1,0:T(1,128)S(1)}, u32[]{:S(2)}, u32[]{:S(2)}) async-start(f32[8,1,2048]{2,1,0:T(1,128)} %stack.12), calls=%async_computation | async-start | bytes 131072 | tf_op jit(solution)/shard_map/all_to_all | solution.py:188
  14.3 1.3 fusion.78
  15.7 1.3 exponential_bitcast_fusion
  19.5 1.3 fusion.76
  20.8 39.2 %all-gather.2 = f32[32,1,512]{2,1,0:T(1,128)S(1)} all-gather(f32[1,1,512]{2,1,0:T(1,128)S(1)} %exponential_bitcast_fusion), channel_id=1, replica_groups=mesh['slab'=32,'mode'=8] {'slab'}, dimensions={0}, use_global_device_ids=true | all-gather | bytes 67584 | tf_op jit(solution)/shard_map/all_gather | solution.py:16
  60.0 26.2 %all_gather.21 = f32[3,16384]{1,0:T(4,128)S(1)} all-gather(f32[3,2048]{1,0:T(4,128)} %param.12), channel_id=1, replica_groups=mesh['slab'=32,'mode'=8] {'mode'}, dimensions={1}, use_global_device_ids=true | all-gather | bytes 221184 | tf_op jit(solution)/shard_map/all_gather | solution.py:186
  86.9 161.1 %while.60 = (s32[]{:T(128)}, f32[8,4,512,4]{2,3,1,0:T(4,128)S(1)}, f32[8,2048]{1,0:T(8,128)S(1)}, f32[8,3,2048]{2,1,0:T(4,128)S(1)}, f32[]{:T(128)}, /*index=5*/...) while((s32[]{:T(128)}, f32[8,4,512,4]{2,3,1,0:T(4,128)S(1)}, ...), condition=%wide.region_3.4_spmd.clone.clone, body=%wide.region_1.3_spmd.clone.clone.sunk | while | flops 29384708 | bytes 33853620 | solution.py:114
  87.1 1.3 sqrt_negate_fusion.4
  88.4 17.2 %fusion.90 = (f32[1,512,4,512]{3,1,2,0:T(8,128)S(1)}, f32[1,512,4,512]{3,1,2,0:T(8,128)S(1)}, f32[1,512,4,512]{3,1,2,0:T(8,128)S(1)}, f32[1,512,4,512]{3,1,2,0:T(8,128)S(1)}) fusion(f32[4,512]{1,0:T(4,128)S(1)} %mul.1380, f32[512]{0:T(512)S(1)} %get-tuple-element.909, f32[4,512]{1,0:T(4,128)S(1)} %mul.1381, f32[512]{0:T(512)S(1)} %get-tuple-element.911, ...), kind=kLoop, calls=%fused_computation.21.clone.1 | loop fusion | flops 12582912 | bytes 16824320 | tf_op jit(solution)/shard_map/while/body/eval_jaxpr/mul | solution.py:58
  105.6 1.4 maximum_reduce_fusion.2
  107.2 1.3 sqrt_negate_fusion.4
  108.5 17.2 %fusion.90 = (f32[1,512,4,512]{3,1,2,0:T(8,128)S(1)}, f32[1,512,4,512]{3,1,2,0:T(8,128)S(1)}, f32[1,512,4,512]{3,1,2,0:T(8,128)S(1)}, f32[1,512,4,512]{3,1,2,0:T(8,128)S(1)}) fusion(f32[4,512]{1,0:T(4,128)S(1)} %mul.1380, f32[512]{0:T(512)S(1)} %get-tuple-element.909, f32[4,512]{1,0:T(4,128)S(1)} %mul.1381, f32[512]{0:T(512)S(1)} %get-tuple-element.911, ...), kind=kLoop, calls=%fused_computation.21.clone.1 | loop fusion | flops 12582912 | bytes 16824320 | tf_op jit(solution)/shard_map/while/body/eval_jaxpr/mul | solution.py:58
  125.7 1.4 maximum_reduce_fusion.2
  127.4 1.3 sqrt_negate_fusion.4
  128.7 17.2 %fusion.90 = (f32[1,512,4,512]{3,1,2,0:T(8,128)S(1)}, f32[1,512,4,512]{3,1,2,0:T(8,128)S(1)}, f32[1,512,4,512]{3,1,2,0:T(8,128)S(1)}, f32[1,512,4,512]{3,1,2,0:T(8,128)S(1)}) fusion(f32[4,512]{1,0:T(4,128)S(1)} %mul.1380, f32[512]{0:T(512)S(1)} %get-tuple-element.909, f32[4,512]{1,0:T(4,128)S(1)} %mul.1381, f32[512]{0:T(512)S(1)} %get-tuple-element.911, ...), kind=kLoop, calls=%fused_computation.21.clone.1 | loop fusion | flops 12582912 | bytes 16824320 | tf_op jit(solution)/shard_map/while/body/eval_jaxpr/mul | solution.py:58
  145.8 1.4 maximum_reduce_fusion.2
  147.5 1.3 sqrt_negate_fusion.4
  148.8 17.2 %fusion.90 = (f32[1,512,4,512]{3,1,2,0:T(8,128)S(1)}, f32[1,512,4,512]{3,1,2,0:T(8,128)S(1)}, f32[1,512,4,512]{3,1,2,0:T(8,128)S(1)}, f32[1,512,4,512]{3,1,2,0:T(8,128)S(1)}) fusion(f32[4,512]{1,0:T(4,128)S(1)} %mul.1380, f32[512]{0:T(512)S(1)} %get-tuple-element.909, f32[4,512]{1,0:T(4,128)S(1)} %mul.1381, f32[512]{0:T(512)S(1)} %get-tuple-element.911, ...), kind=kLoop, calls=%fused_computation.21.clone.1 | loop fusion | flops 12582912 | bytes 16824320 | tf_op jit(solution)/shard_map/while/body/eval_jaxpr/mul | solution.py:58
  166.0 1.4 maximum_reduce_fusion.2
  167.6 1.3 sqrt_negate_fusion.4
  168.9 17.2 %fusion.90 = (f32[1,512,4,512]{3,1,2,0:T(8,128)S(1)}, f32[1,512,4,512]{3,1,2,0:T(8,128)S(1)}, f32[1,512,4,512]{3,1,2,0:T(8,128)S(1)}, f32[1,512,4,512]{3,1,2,0:T(8,128)S(1)}) fusion(f32[4,512]{1,0:T(4,128)S(1)} %mul.1380, f32[512]{0:T(512)S(1)} %get-tuple-element.909, f32[4,512]{1,0:T(4,128)S(1)} %mul.1381, f32[512]{0:T(512)S(1)} %get-tuple-element.911, ...), kind=kLoop, calls=%fused_computation.21.clone.1 | loop fusion | flops 12582912 | bytes 16824320 | tf_op jit(solution)/shard_map/while/body/eval_jaxpr/mul | solution.py:58
  186.1 1.4 maximum_reduce_fusion.2
  187.8 1.3 sqrt_negate_fusion.4
  189.1 17.2 %fusion.90 = (f32[1,512,4,512]{3,1,2,0:T(8,128)S(1)}, f32[1,512,4,512]{3,1,2,0:T(8,128)S(1)}, f32[1,512,4,512]{3,1,2,0:T(8,128)S(1)}, f32[1,512,4,512]{3,1,2,0:T(8,128)S(1)}) fusion(f32[4,512]{1,0:T(4,128)S(1)} %mul.1380, f32[512]{0:T(512)S(1)} %get-tuple-element.909, f32[4,512]{1,0:T(4,128)S(1)} %mul.1381, f32[512]{0:T(512)S(1)} %get-tuple-element.911, ...), kind=kLoop, calls=%fused_computation.21.clone.1 | loop fusion | flops 12582912 | bytes 16824320 | tf_op jit(solution)/shard_map/while/body/eval_jaxpr/mul | solution.py:58
  206.3 1.4 maximum_reduce_fusion.2
  207.9 1.3 sqrt_negate_fusion.4
  209.2 17.2 %fusion.90 = (f32[1,512,4,512]{3,1,2,0:T(8,128)S(1)}, f32[1,512,4,512]{3,1,2,0:T(8,128)S(1)}, f32[1,512,4,512]{3,1,2,0:T(8,128)S(1)}, f32[1,512,4,512]{3,1,2,0:T(8,128)S(1)}) fusion(f32[4,512]{1,0:T(4,128)S(1)} %mul.1380, f32[512]{0:T(512)S(1)} %get-tuple-element.909, f32[4,512]{1,0:T(4,128)S(1)} %mul.1381, f32[512]{0:T(512)S(1)} %get-tuple-element.911, ...), kind=kLoop, calls=%fused_computation.21.clone.1 | loop fusion | flops 12582912 | bytes 16824320 | tf_op jit(solution)/shard_map/while/body/eval_jaxpr/mul | solution.py:58
  226.4 1.4 maximum_reduce_fusion.2
  228.1 1.3 sqrt_negate_fusion.4
  229.3 17.2 %fusion.90 = (f32[1,512,4,512]{3,1,2,0:T(8,128)S(1)}, f32[1,512,4,512]{3,1,2,0:T(8,128)S(1)}, f32[1,512,4,512]{3,1,2,0:T(8,128)S(1)}, f32[1,512,4,512]{3,1,2,0:T(8,128)S(1)}) fusion(f32[4,512]{1,0:T(4,128)S(1)} %mul.1380, f32[512]{0:T(512)S(1)} %get-tuple-element.909, f32[4,512]{1,0:T(4,128)S(1)} %mul.1381, f32[512]{0:T(512)S(1)} %get-tuple-element.911, ...), kind=kLoop, calls=%fused_computation.21.clone.1 | loop fusion | flops 12582912 | bytes 16824320 | tf_op jit(solution)/shard_map/while/body/eval_jaxpr/mul | solution.py:58
  246.5 1.4 maximum_reduce_fusion.2
  248.1 32.2 %all-gather.3 = f32[32,2,512]{2,1,0:T(2,128)S(1)} all-gather(f32[1,2,512]{2,1,0:T(2,128)S(1)} %get-tuple-element.719), channel_id=2, replica_groups=mesh['slab'=32,'mode'=8] {'slab'}, dimensions={0}, use_global_device_ids=true | all-gather | bytes 135168 | tf_op jit(solution)/shard_map/all_gather | solution.py:16
  280.3 1.8 while.58
  282.3 31.2 %all-gather.4 = f32[32,2,512]{2,1,0:T(2,128)S(1)} all-gather(f32[1,2,512]{2,1,0:T(2,128)S(1)} %get-tuple-element.720), channel_id=3, replica_groups=mesh['slab'=32,'mode'=8] {'slab'}, dimensions={0}, use_global_device_ids=true | all-gather | bytes 135168 | tf_op jit(solution)/shard_map/all_gather | solution.py:16
  313.5 2.3 while.59
  316.4 178.1 %while.61 = (s32[]{:T(128)}, f32[8,3,2048]{2,1,0:T(4,128)S(1)}, f32[8,3,2048]{2,1,0:T(4,128)S(1)}, f32[]{:T(128)}, f32[8,4,512,4]{2,3,1,0:T(4,128)S(1)}, /*index...) while((s32[]{:T(128)}, f32[8,3,2048]{2,1,0:T(4,128)S(1)}, ...), condition=%wide.region_13.14_spmd.clone.clone, body=%wide.region_9.13_spmd.clone.clone.sunk | while | flops 26279428 | bytes 422137 | solution.py:137
  316.5 1.2 multiply_divide_fusion.3
  317.8 1.3 sqrt_negate_fusion.5
  319.1 19.4 %multiply_reduce_fusion.3 = (f32[4,512]{1,0:T(4,128)S(1)}, f32[4,512]{1,0:T(4,128)S(1)}, f32[4,512]{1,0:T(4,128)S(1)}) fusion(f32[512,4]{0,1:T(4,128)S(1)} %get-tuple-element.927, f32[512,4]{0,1:T(4,128)S(1)} %get-tuple-element.928, f32[512,4]{0,1:T(4,128)S(1)} %get-tuple-element.929, f32[4,512]{1,0:T(4,128)S(1)} %broadcast_subtract_fusion.5, ...), kind=kLoop, calls=%fused_computation.59.clone.1 | loop fusion | flops 26208256 | bytes 100352 | tf_op jit(solution)/shard_map/while/body/eval_jaxpr/reduce_sum | solution.py:85
  338.8 1.2 multiply_divide_fusion.3
  340.0 1.3 sqrt_negate_fusion.5
  341.3 19.4 %multiply_reduce_fusion.3 = (f32[4,512]{1,0:T(4,128)S(1)}, f32[4,512]{1,0:T(4,128)S(1)}, f32[4,512]{1,0:T(4,128)S(1)}) fusion(f32[512,4]{0,1:T(4,128)S(1)} %get-tuple-element.927, f32[512,4]{0,1:T(4,128)S(1)} %get-tuple-element.928, f32[512,4]{0,1:T(4,128)S(1)} %get-tuple-element.929, f32[4,512]{1,0:T(4,128)S(1)} %broadcast_subtract_fusion.5, ...), kind=kLoop, calls=%fused_computation.59.clone.1 | loop fusion | flops 26208256 | bytes 100352 | tf_op jit(solution)/shard_map/while/body/eval_jaxpr/reduce_sum | solution.py:85
  361.1 1.2 multiply_divide_fusion.3
  362.3 1.3 sqrt_negate_fusion.5
  363.6 19.4 %multiply_reduce_fusion.3 = (f32[4,512]{1,0:T(4,128)S(1)}, f32[4,512]{1,0:T(4,128)S(1)}, f32[4,512]{1,0:T(4,128)S(1)}) fusion(f32[512,4]{0,1:T(4,128)S(1)} %get-tuple-element.927, f32[512,4]{0,1:T(4,128)S(1)} %get-tuple-element.928, f32[512,4]{0,1:T(4,128)S(1)} %get-tuple-element.929, f32[4,512]{1,0:T(4,128)S(1)} %broadcast_subtract_fusion.5, ...), kind=kLoop, calls=%fused_computation.59.clone.1 | loop fusion | flops 26208256 | bytes 100352 | tf_op jit(solution)/shard_map/while/body/eval_jaxpr/reduce_sum | solution.py:85
  383.3 1.2 multiply_divide_fusion.3
  384.6 1.3 sqrt_negate_fusion.5
  385.9 19.4 %multiply_reduce_fusion.3 = (f32[4,512]{1,0:T(4,128)S(1)}, f32[4,512]{1,0:T(4,128)S(1)}, f32[4,512]{1,0:T(4,128)S(1)}) fusion(f32[512,4]{0,1:T(4,128)S(1)} %get-tuple-element.927, f32[512,4]{0,1:T(4,128)S(1)} %get-tuple-element.928, f32[512,4]{0,1:T(4,128)S(1)} %get-tuple-element.929, f32[4,512]{1,0:T(4,128)S(1)} %broadcast_subtract_fusion.5, ...), kind=kLoop, calls=%fused_computation.59.clone.1 | loop fusion | flops 26208256 | bytes 100352 | tf_op jit(solution)/shard_map/while/body/eval_jaxpr/reduce_sum | solution.py:85
  405.6 1.2 multiply_divide_fusion.3
  406.8 1.3 sqrt_negate_fusion.5
  408.1 19.4 %multiply_reduce_fusion.3 = (f32[4,512]{1,0:T(4,128)S(1)}, f32[4,512]{1,0:T(4,128)S(1)}, f32[4,512]{1,0:T(4,128)S(1)}) fusion(f32[512,4]{0,1:T(4,128)S(1)} %get-tuple-element.927, f32[512,4]{0,1:T(4,128)S(1)} %get-tuple-element.928, f32[512,4]{0,1:T(4,128)S(1)} %get-tuple-element.929, f32[4,512]{1,0:T(4,128)S(1)} %broadcast_subtract_fusion.5, ...), kind=kLoop, calls=%fused_computation.59.clone.1 | loop fusion | flops 26208256 | bytes 100352 | tf_op jit(solution)/shard_map/while/body/eval_jaxpr/reduce_sum | solution.py:85
  427.9 1.2 multiply_divide_fusion.3
  429.1 1.3 sqrt_negate_fusion.5
  430.4 19.4 %multiply_reduce_fusion.3 = (f32[4,512]{1,0:T(4,128)S(1)}, f32[4,512]{1,0:T(4,128)S(1)}, f32[4,512]{1,0:T(4,128)S(1)}) fusion(f32[512,4]{0,1:T(4,128)S(1)} %get-tuple-element.927, f32[512,4]{0,1:T(4,128)S(1)} %get-tuple-element.928, f32[512,4]{0,1:T(4,128)S(1)} %get-tuple-element.929, f32[4,512]{1,0:T(4,128)S(1)} %broadcast_subtract_fusion.5, ...), kind=kLoop, calls=%fused_computation.59.clone.1 | loop fusion | flops 26208256 | bytes 100352 | tf_op jit(solution)/shard_map/while/body/eval_jaxpr/reduce_sum | solution.py:85
  450.1 1.2 multiply_divide_fusion.3
  451.4 1.3 sqrt_negate_fusion.5
  452.7 19.4 %multiply_reduce_fusion.3 = (f32[4,512]{1,0:T(4,128)S(1)}, f32[4,512]{1,0:T(4,128)S(1)}, f32[4,512]{1,0:T(4,128)S(1)}) fusion(f32[512,4]{0,1:T(4,128)S(1)} %get-tuple-element.927, f32[512,4]{0,1:T(4,128)S(1)} %get-tuple-element.928, f32[512,4]{0,1:T(4,128)S(1)} %get-tuple-element.929, f32[4,512]{1,0:T(4,128)S(1)} %broadcast_subtract_fusion.5, ...), kind=kLoop, calls=%fused_computation.59.clone.1 | loop fusion | flops 26208256 | bytes 100352 | tf_op jit(solution)/shard_map/while/body/eval_jaxpr/reduce_sum | solution.py:85
  472.4 1.2 multiply_divide_fusion.3
  473.6 1.3 sqrt_negate_fusion.5
  474.9 19.4 %multiply_reduce_fusion.3 = (f32[4,512]{1,0:T(4,128)S(1)}, f32[4,512]{1,0:T(4,128)S(1)}, f32[4,512]{1,0:T(4,128)S(1)}) fusion(f32[512,4]{0,1:T(4,128)S(1)} %get-tuple-element.927, f32[512,4]{0,1:T(4,128)S(1)} %get-tuple-element.928, f32[512,4]{0,1:T(4,128)S(1)} %get-tuple-element.929, f32[4,512]{1,0:T(4,128)S(1)} %broadcast_subtract_fusion.5, ...), kind=kLoop, calls=%fused_computation.59.clone.1 | loop fusion | flops 26208256 | bytes 100352 | tf_op jit(solution)/shard_map/while/body/eval_jaxpr/reduce_sum | solution.py:85
  494.5 5.1 copy.33
  499.6 71.1 %reduce-scatter.4.cloned.1.call-done = f32[2048,3]{1,0:T(8,128)} async-done(((f32[16384,3]{1,0:T(8,128)}), f32[2048,3]{1,0:T(8,128)}) %reduce-scatter.4.cloned.1.call-update) | async-done | bytes 24592
  570.7 2.2 copy.34
  (318 shorter events, 8.0 us)
Async XLA Ops:
  7.9 78.3 %all-to-all-start = ((f32[8,1,2048]{2,1,0:T(1,128)}), f32[8,1,2048]{2,1,0:T(1,128)S(1)}, u32[]{:S(2)}, u32[]{:S(2)}) async-start(f32[8,1,2048]{2,1,0:T(1,128)} %stack.12), calls=%async_computation | async-start | bytes 131072 | tf_op jit(solution)/shard_map/all_to_all | solution.py:188
  14.3 556.4 %reduce-scatter.4.cloned.1.call-start = ((), (), s32[]{:S(2)}) async-start(), calls=%async_computation.2 | async-start | bytes 9437184
Sparse Core Ops, SparseCore 0:
  499.7 70.9 reduce-scatter.3
